TPU v7x, 32 devices: a whole 2x2x4 slice. The times are simulated.
32 devices in a mesh: dp: 4 (over y, x), ctx: 8 (over z, core).
Axes of the slice: x: 2, y: 2, z: 4, core: 2. Of those that a mesh axis runs over, the one named last changes fastest.
Arguments:
- queries: bfloat16 [4096, 64, 128], P(('dp', 'ctx')), parts along dimension 0, may hold values from -4.5 to 4.5
- keys: bfloat16 [4096, 8, 128], P(('dp', 'ctx')), parts along dimension 0, may hold values from -4.5 to 4.5
- values: bfloat16 [4096, 8, 128], P(('dp', 'ctx')), parts along dimension 0, may hold values from -6 to 6
- out_grad: bfloat16 [4096, 64, 128], P(('dp', 'ctx')), parts along dimension 0, may hold values from -48 to 48
- rand_blocks: int32 [256, 16, 3], P(('dp', 'ctx')), parts along dimension 0, may hold values from 0 to 15, as said below
- global_blocks: int32 [8], P('dp'), parts along dimension 0, may hold values from 0 to 15, as said below
Outputs:
- output: bfloat16 [4096, 64, 128], P(('dp', 'ctx')), parts along dimension 0
- query_grad: bfloat16 [4096, 64, 128], P(('dp', 'ctx')), parts along dimension 0
- key_grad: bfloat16 [4096, 8, 128], P(('dp', 'ctx')), parts along dimension 0
- value_grad: bfloat16 [4096, 8, 128], P(('dp', 'ctx')), parts along dimension 0
There are 4 independent parts, one for each index of `dp`. A program takes and returns all parts, laid end to end along the dimension named above; each array names one. Nothing has to cross between parts.
Inputs may be any that keep to these rules, and one draw needn't show every extreme that they name: `rand_blocks`: for each query head and query block, 3 different blocks, none of them the query block or a block beside it (modulo 16), none of them a global block. `global_blocks`: 2 different blocks.
All inputs are finite; a program needn't handle non-finite values.
Results may differ from a plain program's by a relative error of at most 0.011.
Values may be sent and summed in bfloat16 or wider, within the bound.
A program may use at most 192 MiB of HBM per device.

v0:
```python
from functools import partial
import math

import jax
import jax.numpy as jnp
from jax import lax
from jax.sharding import PartitionSpec as P

BLK = 64


def block_table(rand_head, global_blocks, block_count):
    row_ids = jnp.arange(block_count, dtype=jnp.int32)
    window = jnp.stack(
        [(row_ids + block_count - 1) % block_count, row_ids, (row_ids + 1) % block_count], axis=1
    )
    glob_cols = jnp.broadcast_to(global_blocks[None, :], (block_count, global_blocks.shape[0]))
    key_table = jnp.concatenate([window, glob_cols, rand_head], axis=1)
    slot_count = key_table.shape[1]
    repeated = key_table[:, :, None] == key_table[:, None, :]
    earlier = jnp.arange(slot_count)[None, :] < jnp.arange(slot_count)[:, None]
    usable = jnp.logical_not(jnp.any(jnp.logical_and(repeated, earlier[None, :, :]), axis=2))
    return (key_table, usable)


def group_size(block_count, block_rows):
    return math.gcd(block_count, max(1, 512 // block_rows))


def contract(form, left, right):
    return jnp.einsum(form, left, right, preferred_element_type=jnp.float32)


def forward_head(global_blocks, operands):
    query_h, key_h, value_h, rand_head = operands
    length, head_width = query_h.shape
    block_count = length // BLK
    per_step = group_size(block_count, BLK)
    step_count = block_count // per_step
    key_table, usable = block_table(rand_head, global_blocks, block_count)
    factor = 1.0 / math.sqrt(head_width)
    key_full = key_h.reshape(block_count, BLK, head_width)[key_table]
    value_full = value_h.reshape(block_count, BLK, head_width)[key_table]
    slot_count = key_table.shape[1]
    packs = (
        query_h.reshape(step_count, per_step, BLK, head_width),
        key_full.reshape(step_count, per_step, slot_count * BLK, head_width),
        value_full.reshape(step_count, per_step, slot_count * BLK, head_width),
        usable.reshape(step_count, per_step, -1),
    )

    def forward_one_group(group_pack):
        query_g, key_g, value_g, usable_g = group_pack
        scores = contract("abd,akd->abk", query_g, key_g) * factor
        live_cols = jnp.repeat(usable_g, BLK, axis=1)[:, None, :]
        scores = jnp.where(live_cols, scores, -jnp.inf)
        row_max = jnp.max(scores, axis=2, keepdims=True)
        raw_weight = jnp.exp(scores - row_max)
        prob_rows = (raw_weight / jnp.sum(raw_weight, axis=2, keepdims=True)).astype(jnp.bfloat16)
        result = contract("abk,akd->abd", prob_rows, value_g).astype(jnp.bfloat16)
        return (result, prob_rows)

    result, prob_rows = lax.map(forward_one_group, packs)
    return (result.reshape(length, head_width), prob_rows, key_full, value_full)


def backward_head(global_blocks, operands):
    query_h, grad_h, out_h, prob_all, key_full, value_full, rand_head = operands
    length, head_width = query_h.shape
    block_count = length // BLK
    per_step = group_size(block_count, BLK)
    step_count = block_count // per_step
    key_table, usable = block_table(rand_head, global_blocks, block_count)
    slot_count = key_table.shape[1]
    factor = 1.0 / math.sqrt(head_width)
    delta_all = jnp.sum(grad_h.astype(jnp.float32) * out_h.astype(jnp.float32), axis=1)
    packs = (
        query_h.reshape(step_count, per_step, BLK, head_width),
        grad_h.reshape(step_count, per_step, BLK, head_width),
        delta_all.reshape(step_count, per_step, BLK),
        prob_all,
        key_full.reshape(step_count, per_step, slot_count * BLK, head_width),
        value_full.reshape(step_count, per_step, slot_count * BLK, head_width),
        key_table.reshape(step_count, per_step, slot_count),
    )

    def backward_one_group(carry, group_pack):
        key_acc, value_acc = carry
        query_g, grad_g, delta_g, prob_g, key_g, value_g, table_g = group_pack
        value_part = contract("abk,abd->akd", prob_g, grad_g)
        dprob = contract("abd,akd->abk", grad_g, value_g)
        dscore = (prob_g.astype(jnp.float32) * (dprob - delta_g[:, :, None])).astype(jnp.bfloat16)
        query_grad = (contract("abk,akd->abd", dscore, key_g) * factor).astype(jnp.bfloat16)
        key_part = contract("abk,abd->akd", dscore, query_g) * factor
        flat_ids = table_g.reshape(-1)
        key_acc = key_acc.at[flat_ids].add(key_part.reshape(-1, BLK, head_width))
        value_acc = value_acc.at[flat_ids].add(value_part.reshape(-1, BLK, head_width))
        return ((key_acc, value_acc), query_grad)

    zeros_acc = jnp.zeros((block_count, BLK, head_width), jnp.float32)
    (key_acc, value_acc), query_grad = lax.scan(backward_one_group, (zeros_acc, zeros_acc), packs)
    return (
        query_grad.reshape(length, head_width),
        key_acc.reshape(length, head_width).astype(jnp.bfloat16),
        value_acc.reshape(length, head_width).astype(jnp.bfloat16),
    )


def heads_first(array):
    return jnp.moveaxis(array, 1, 0)


def tokens_first(array):
    return jnp.moveaxis(array, 0, 1)


def body(queries, keys, values, out_grad, rand_blocks, global_blocks):
    head_total = queries.shape[1]
    kv_total = keys.shape[1]
    heads_per_kv = head_total // kv_total
    keys_wide = jnp.repeat(keys, heads_per_kv, axis=1)
    values_wide = jnp.repeat(values, heads_per_kv, axis=1)
    query_heads, key_heads, value_heads = (
        lax.all_to_all(queries, "ctx", split_axis=1, concat_axis=0, tiled=True),
        lax.all_to_all(keys_wide, "ctx", split_axis=1, concat_axis=0, tiled=True),
        lax.all_to_all(values_wide, "ctx", split_axis=1, concat_axis=0, tiled=True),
    )
    query_lead = heads_first(query_heads)
    key_lead = heads_first(key_heads)
    value_lead = heads_first(value_heads)
    out_heads, prob_heads, key_fulls, value_fulls = lax.map(
        partial(forward_head, global_blocks), (query_lead, key_lead, value_lead, rand_blocks)
    )
    out_seq = tokens_first(out_heads)
    output = lax.all_to_all(out_seq, "ctx", split_axis=0, concat_axis=1, tiled=True)
    grad_heads = lax.all_to_all(out_grad, "ctx", split_axis=1, concat_axis=0, tiled=True)
    query_parts, key_parts, value_parts = lax.map(
        partial(backward_head, global_blocks),
        (
            query_lead,
            heads_first(grad_heads),
            out_heads,
            prob_heads,
            key_fulls,
            value_fulls,
            rand_blocks,
        ),
    )
    query_seq = tokens_first(query_parts)
    key_seq = tokens_first(key_parts)
    value_seq = tokens_first(value_parts)
    query_back, key_back, value_back = (
        lax.all_to_all(query_seq, "ctx", split_axis=0, concat_axis=1, tiled=True),
        lax.all_to_all(key_seq, "ctx", split_axis=0, concat_axis=1, tiled=True),
        lax.all_to_all(value_seq, "ctx", split_axis=0, concat_axis=1, tiled=True),
    )
    tokens_here = query_back.shape[0]
    head_width = query_back.shape[2]
    key_grad = (
        key_back.reshape(tokens_here, kv_total, heads_per_kv, head_width)
        .astype(jnp.float32)
        .sum(axis=2)
        .astype(jnp.bfloat16)
    )
    value_grad = (
        value_back.reshape(tokens_here, kv_total, heads_per_kv, head_width)
        .astype(jnp.float32)
        .sum(axis=2)
        .astype(jnp.bfloat16)
    )
    return (output, query_back, key_grad, value_grad)


def solution(mesh):
    return jax.shard_map(
        body,
        mesh=mesh,
        in_specs=(
            P(("dp", "ctx"), None, None),
            P(("dp", "ctx"), None, None),
            P(("dp", "ctx"), None, None),
            P(("dp", "ctx"), None, None),
            P(("dp", "ctx"), None, None),
            P("dp"),
        ),
        out_specs=(
            P(("dp", "ctx"), None, None),
            P(("dp", "ctx"), None, None),
            P(("dp", "ctx"), None, None),
            P(("dp", "ctx"), None, None),
        ),
        check_vma=False,
    )
```

profile of v0, /device:TPU:0, one launch (start us, length us, event | category | flops | bytes accessed | tf_op | source)
XLA Modules:
  0.0 953.6 jit_solution(9236519392290810154)
XLA Ops:
  4.9 6.5 all-to-all-start
  11.4 49.0 %all-to-all-done = bf16[128,64,128]{2,0,1:T(8,128)(2,1)S(1)} async-done(((bf16[128,64,128]{2,0,1:T(8,128)(2,1)}), bf16[128,64,128]{2,0,1:T(8,128)(2,1)S(1)}, u32[]{:S(2)}, u32[]{:S(2)}) %all-to-all-start) | async-done | bytes 2097184 | tf_op jit(solution)/shard_map/all_to_all | solution.py:124
  62.3 4.5 all-to-all-start.1
  66.8 49.0 %all-to-all-done.1 = bf16[128,64,128]{2,0,1:T(8,128)(2,1)} async-done(((bf16[128,64,128]{2,0,1:T(8,128)(2,1)}), bf16[128,64,128]{2,0,1:T(8,128)(2,1)}, u32[]{:S(2)}, u32[]{:S(2)}) %all-to-all-start.1) | async-done | bytes 2097184 | tf_op jit(solution)/shard_map/all_to_all | solution.py:125
  117.7 4.4 all-to-all-start.2
  132.5 38.6 %all-to-all-done.2 = bf16[128,64,128]{2,0,1:T(8,128)(2,1)} async-done(((bf16[128,64,128]{2,0,1:T(8,128)(2,1)}), bf16[128,64,128]{2,0,1:T(8,128)(2,1)}, u32[]{:S(2)}, u32[]{:S(2)}) %all-to-all-start.2) | async-done | bytes 2097184 | tf_op jit(solution)/shard_map/all_to_all | solution.py:126
  171.1 4.5 all-to-all-start.4
  181.8 181.9 %while.119 = (s32[]{:T(128)}, bf16[8,1024,128]{2,1,0:T(8,128)(2,1)}, bf16[8,2,8,64,512]{4,3,2,1,0:T(8,128)(2,1)}, bf16[8,16,8,64,128]{4,3,2,1,0:T(8,128)(2,1)}, ...) while((s32[]{:T(128)}, bf16[8,1024,128]{2,1,0:T(8,128)(2,1)}, ...), condition=%wide.region_6.7_spmd, body=%wide.region_0.6_spmd.sunk | while | flops 136386240 | bytes 35434640 | solution.py:131
  189.2 8.1 while.122
  211.9 8.1 while.122
  234.7 8.1 while.122
  257.4 8.1 while.122
  280.3 8.1 while.122
  303.0 8.1 while.122
  325.7 8.1 while.122
  348.5 8.1 while.122
  371.8 359.5 %while.121 = (s32[]{:T(128)}, bf16[8,1024,128]{2,1,0:T(8,128)(2,1)}, bf16[8,1024,128]{2,1,0:T(8,128)(2,1)}, bf16[8,1024,128]{2,1,0:T(8,128)(2,1)}, bf16[8,1024,1...) while((s32[]{:T(128)}, bf16[8,1024,128]{2,1,0:T(8,128)(2,1)}, ...), condition=%wide.region_13.14_spmd, body=%wide.region_7.13_spmd.sunk | while | flops 271974048 | bytes 42508404 | solution.py:137
  385.4 29.6 %while.123 = (s32[]{:T(128)}, f32[16,64,128]{2,1,0:T(8,128)S(1)}, f32[16,64,128]{2,1,0:T(8,128)S(1)}, bf16[2,8,64,128]{3,2,1,0:T(8,128)(2,1)}, s32[2,8,8]{1,0,2:...) while((s32[]{:T(128)}, f32[16,64,128]{2,1,0:T(8,128)S(1)}, ...), condition=%wide.region_12.12_spmd, body=%wide.region_9.11_spmd.sunk | while | flops 271188160 | bytes 25180344 | solution.py:101
  430.3 29.6 %while.123 = (s32[]{:T(128)}, f32[16,64,128]{2,1,0:T(8,128)S(1)}, f32[16,64,128]{2,1,0:T(8,128)S(1)}, bf16[2,8,64,128]{3,2,1,0:T(8,128)(2,1)}, s32[2,8,8]{1,0,2:...) while((s32[]{:T(128)}, f32[16,64,128]{2,1,0:T(8,128)S(1)}, ...), condition=%wide.region_12.12_spmd, body=%wide.region_9.11_spmd.sunk | while | flops 271188160 | bytes 25180344 | solution.py:101
  475.3 29.6 %while.123 = (s32[]{:T(128)}, f32[16,64,128]{2,1,0:T(8,128)S(1)}, f32[16,64,128]{2,1,0:T(8,128)S(1)}, bf16[2,8,64,128]{3,2,1,0:T(8,128)(2,1)}, s32[2,8,8]{1,0,2:...) while((s32[]{:T(128)}, f32[16,64,128]{2,1,0:T(8,128)S(1)}, ...), condition=%wide.region_12.12_spmd, body=%wide.region_9.11_spmd.sunk | while | flops 271188160 | bytes 25180344 | solution.py:101
  520.2 29.6 %while.123 = (s32[]{:T(128)}, f32[16,64,128]{2,1,0:T(8,128)S(1)}, f32[16,64,128]{2,1,0:T(8,128)S(1)}, bf16[2,8,64,128]{3,2,1,0:T(8,128)(2,1)}, s32[2,8,8]{1,0,2:...) while((s32[]{:T(128)}, f32[16,64,128]{2,1,0:T(8,128)S(1)}, ...), condition=%wide.region_12.12_spmd, body=%wide.region_9.11_spmd.sunk | while | flops 271188160 | bytes 25180344 | solution.py:101
  565.1 29.6 %while.123 = (s32[]{:T(128)}, f32[16,64,128]{2,1,0:T(8,128)S(1)}, f32[16,64,128]{2,1,0:T(8,128)S(1)}, bf16[2,8,64,128]{3,2,1,0:T(8,128)(2,1)}, s32[2,8,8]{1,0,2:...) while((s32[]{:T(128)}, f32[16,64,128]{2,1,0:T(8,128)S(1)}, ...), condition=%wide.region_12.12_spmd, body=%wide.region_9.11_spmd.sunk | while | flops 271188160 | bytes 25180344 | solution.py:101
  610.1 29.6 %while.123 = (s32[]{:T(128)}, f32[16,64,128]{2,1,0:T(8,128)S(1)}, f32[16,64,128]{2,1,0:T(8,128)S(1)}, bf16[2,8,64,128]{3,2,1,0:T(8,128)(2,1)}, s32[2,8,8]{1,0,2:...) while((s32[]{:T(128)}, f32[16,64,128]{2,1,0:T(8,128)S(1)}, ...), condition=%wide.region_12.12_spmd, body=%wide.region_9.11_spmd.sunk | while | flops 271188160 | bytes 25180344 | solution.py:101
  655.0 29.6 %while.123 = (s32[]{:T(128)}, f32[16,64,128]{2,1,0:T(8,128)S(1)}, f32[16,64,128]{2,1,0:T(8,128)S(1)}, bf16[2,8,64,128]{3,2,1,0:T(8,128)(2,1)}, s32[2,8,8]{1,0,2:...) while((s32[]{:T(128)}, f32[16,64,128]{2,1,0:T(8,128)S(1)}, ...), condition=%wide.region_12.12_spmd, body=%wide.region_9.11_spmd.sunk | while | flops 271188160 | bytes 25180344 | solution.py:101
  700.0 29.6 %while.123 = (s32[]{:T(128)}, f32[16,64,128]{2,1,0:T(8,128)S(1)}, f32[16,64,128]{2,1,0:T(8,128)S(1)}, bf16[2,8,64,128]{3,2,1,0:T(8,128)(2,1)}, s32[2,8,8]{1,0,2:...) while((s32[]{:T(128)}, f32[16,64,128]{2,1,0:T(8,128)S(1)}, ...), condition=%wide.region_12.12_spmd, body=%wide.region_9.11_spmd.sunk | while | flops 271188160 | bytes 25180344 | solution.py:101
  735.5 4.8 all-to-all-start.5
  744.6 44.8 %all-to-all-done.5 = bf16[1024,8,128]{2,1,0:T(8,128)(2,1)S(1)} async-done(((bf16[1024,8,128]{2,1,0:T(8,128)(2,1)}), bf16[1024,8,128]{2,1,0:T(8,128)(2,1)S(1)}, u32[]{:S(2)}, u32[]{:S(2)}) %all-to-all-start.5) | async-done | bytes 2097184 | tf_op jit(solution)/shard_map/all_to_all | solution.py:153
  798.6 44.7 %all-to-all-done.6 = bf16[1024,8,128]{2,1,0:T(8,128)(2,1)S(1)} async-done(((bf16[1024,8,128]{2,1,0:T(8,128)(2,1)}), bf16[1024,8,128]{2,1,0:T(8,128)(2,1)S(1)}, u32[]{:S(2)}, u32[]{:S(2)}) %all-to-all-start.6) | async-done | bytes 2097184 | tf_op jit(solution)/shard_map/all_to_all | solution.py:154
  843.3 4.3 all-to-all-start.7
  851.9 44.8 %all-to-all-done.7 = bf16[1024,8,128]{2,1,0:T(8,128)(2,1)} async-done(((bf16[1024,8,128]{2,1,0:T(8,128)(2,1)}), bf16[1024,8,128]{2,1,0:T(8,128)(2,1)}, u32[]{:S(2)}, u32[]{:S(2)}) %all-to-all-start.7) | async-done | bytes 2097184 | tf_op jit(solution)/shard_map/all_to_all | solution.py:155
  896.7 4.3 all-to-all-start.3
  910.7 39.4 %all-to-all-done.3 = bf16[1024,8,128]{2,1,0:T(8,128)(2,1)} async-done(((bf16[1024,8,128]{2,1,0:T(8,128)(2,1)}), bf16[1024,8,128]{2,1,0:T(8,128)(2,1)}, u32[]{:S(2)}, u32[]{:S(2)}) %all-to-all-start.3) | async-done | bytes 2097184 | tf_op jit(solution)/shard_map/all_to_all | solution.py:135
  (807 shorter events, 606.7 us)
Async XLA Ops:
  4.9 6.5 copy-start.5
  4.9 55.5 %all-to-all-start = ((bf16[128,64,128]{2,0,1:T(8,128)(2,1)}), bf16[128,64,128]{2,0,1:T(8,128)(2,1)S(1)}, u32[]{:S(2)}, u32[]{:S(2)}) async-start(bf16[128,64,128]{2,0,1:T(8,128)(2,1)} %copy.73), calls=%async_computation | async-start | bytes 4194304 | tf_op jit(solution)/shard_map/all_to_all | solution.py:124
  62.3 4.5 copy-start.6
  62.3 53.5 %all-to-all-start.1 = ((bf16[128,64,128]{2,0,1:T(8,128)(2,1)}), bf16[128,64,128]{2,0,1:T(8,128)(2,1)}, u32[]{:S(2)}, u32[]{:S(2)}) async-start(bf16[128,64,128]{2,0,1:T(8,128)(2,1)} %bitcast.253), calls=%async_computation.1 | async-start | bytes 4194304 | tf_op jit(solution)/shard_map/all_to_all | solution.py:125
  117.7 53.4 %all-to-all-start.2 = ((bf16[128,64,128]{2,0,1:T(8,128)(2,1)}), bf16[128,64,128]{2,0,1:T(8,128)(2,1)}, u32[]{:S(2)}, u32[]{:S(2)}) async-start(bf16[128,64,128]{2,0,1:T(8,128)(2,1)} %bitcast.249), calls=%async_computation.2 | async-start | bytes 4194304 | tf_op jit(solution)/shard_map/all_to_all | solution.py:126
  171.1 192.6 %all-to-all-start.4 = ((bf16[128,64,128]{2,0,1:T(8,128)(2,1)}), bf16[128,64,128]{2,0,1:T(8,128)(2,1)}, u32[]{:S(2)}, u32[]{:S(2)}) async-start(bf16[128,64,128]{2,0,1:T(8,128)(2,1)} %copy.85), calls=%async_computation.4 | async-start | bytes 4194304 | tf_op jit(solution)/shard_map/all_to_all | solution.py:136
  197.2 4.1 copy-start.1
  220.0 4.2 copy-start.1
  242.8 4.1 copy-start.1
  265.5 4.2 copy-start.1
  288.3 4.1 copy-start.1
  311.1 4.1 copy-start.1
  333.8 4.1 copy-start.1
  356.5 4.1 copy-start.1
  385.4 2.7 copy-start.2
  400.2 2.7 copy-start.2
  430.4 2.7 copy-start.2
  445.2 2.7 copy-start.2
  475.3 2.7 copy-start.2
  490.1 2.7 copy-start.2
  535.0 2.7 copy-start.2
  565.1 2.7 copy-start.2
  580.0 2.7 copy-start.2
  610.1 2.7 copy-start.2
  624.9 2.7 copy-start.2
  669.9 2.7 copy-start.2
  700.0 2.7 copy-start.2
  714.8 2.7 copy-start.2
  735.5 53.9 %all-to-all-start.5 = ((bf16[1024,8,128]{2,1,0:T(8,128)(2,1)}), bf16[1024,8,128]{2,1,0:T(8,128)(2,1)S(1)}, u32[]{:S(2)}, u32[]{:S(2)}) async-start(bf16[1024,8,128]{2,1,0:T(8,128)(2,1)} %bitcast.252), calls=%async_computation.5 | async-start | bytes 4194304 | tf_op jit(solution)/shard_map/all_to_all | solution.py:153
  790.7 52.6 %all-to-all-start.6 = ((bf16[1024,8,128]{2,1,0:T(8,128)(2,1)}), bf16[1024,8,128]{2,1,0:T(8,128)(2,1)S(1)}, u32[]{:S(2)}, u32[]{:S(2)}) async-start(bf16[1024,8,128]{2,1,0:T(8,128)(2,1)} %bitcast.250), calls=%async_computation.6 | async-start | bytes 4194304 | tf_op jit(solution)/shard_map/all_to_all | solution.py:154
  843.3 53.4 %all-to-all-start.7 = ((bf16[1024,8,128]{2,1,0:T(8,128)(2,1)}), bf16[1024,8,128]{2,1,0:T(8,128)(2,1)}, u32[]{:S(2)}, u32[]{:S(2)}) async-start(bf16[1024,8,128]{2,1,0:T(8,128)(2,1)} %bitcast.251), calls=%async_computation.7 | async-start | bytes 4194304 | tf_op jit(solution)/shard_map/all_to_all | solution.py:155
  896.7 53.4 %all-to-all-start.3 = ((bf16[1024,8,128]{2,1,0:T(8,128)(2,1)}), bf16[1024,8,128]{2,1,0:T(8,128)(2,1)}, u32[]{:S(2)}, u32[]{:S(2)}) async-start(bf16[1024,8,128]{2,1,0:T(8,128)(2,1)} %bitcast.248), calls=%async_computation.3 | async-start | bytes 4194304 | tf_op jit(solution)/shard_map/all_to_all | solution.py:135
  (28 other events, 28.6 us)
where the time goes:
time: 960 us; the launch traced here: 954 us
  waiting for transfers between devices  310 us (32%)
  local copies, waits for them, and re-layouts  305 us (32%)
  other arithmetic  151 us (16%)
  matrix products  147 us (15%)
  starting transfers between devices  37 us (4%)
    dot_general x80, matrix products, contract(): return jnp.einsum(form, left, right, preferred_element_type=jnp.float32)  137 us
    dynamic_update_slice x40, local copies, waits for them, and re-layouts, body(): lax.map(partial(forward_head, global_blocks), (query_lead, key_lead, valu...  70.8 us
    scatter-add x16, other arithmetic, backward_one_group(): key_acc = key_acc.at[flat_ids].add(key_part.reshape(-1, BLK, head_width))  59.7 us
    scatter-add x16, other arithmetic, backward_one_group(): value_acc.at[flat_ids].add(value_part.reshape(-1, BLK, head_width))  59.7 us
    dynamic_slice x16, local copies, waits for them, and re-layouts, body(): lax.map(partial(backward_head, global_blocks), (query_lead, heads_first(g...  50.5 us
    dynamic_slice x56, local copies, waits for them, and re-layouts, body(): lax.map(partial(forward_head, global_blocks), (query_lead, key_lead, valu...  50.2 us
    all_to_all x1, waiting for transfers between devices, body(): lax.all_to_all(queries, 'ctx', split_axis=1, concat_axis=0, tiled=True)  49 us
    all_to_all x1, waiting for transfers between devices, body(): lax.all_to_all(keys_wide, 'ctx', split_axis=1, concat_axis=0, tiled=True)  49 us
  transfers between devices with their start and end apart: 8, of which 7 were waited for; matrix products, arithmetic and copies ran while one was open for 23% of the time, Pallas kernels for 0%

commit v1 on v0

v1 whole, which is shorter than its diff:
```python
import functools
import math

import jax
import jax.numpy as jnp
from jax import lax
from jax.experimental import pallas as pl
from jax.experimental.pallas import tpu as pltpu
from jax.sharding import PartitionSpec as P

BLK = 64
NT = (((1,), (1,)), ((), ()))
NN = (((1,), (0,)), ((), ()))


def dot(left, right, dims=NN):
    return lax.dot_general(left, right, dims, preferred_element_type=jnp.float32)


def flat_rows(block):
    rows = block.shape[0] * block.shape[1]
    return block.astype(jnp.float32).reshape(rows, block.shape[2])


def for_chunks(count, step, init):
    return lax.fori_loop(0, count, step, init, unroll=count <= 4)


def attention(geometry, q_ref, g_ref, kv_ref, bias_ref, out_ref, dq_ref, dkv_ref, s_buf, e_buf, acc):
    chunk, row_tile = geometry
    shards, _, _, shard_tokens, width = kv_ref.shape
    length = shards * shard_tokens
    count = length // chunk
    tokens, group, _ = q_ref.shape
    rows = tokens * group
    tiles = rows // row_tile
    tile_tokens = row_tile // group
    factor = 1.0 / math.sqrt(width)
    to_log2 = factor * math.log2(math.e)
    per_chunk = chunk // shard_tokens

    def kv_chunk(which, c):
        return kv_ref[pl.ds(c * per_chunk, per_chunk), 0, which].reshape(chunk, width)

    for tile in range(tiles):
        t0 = tile * tile_tokens
        lanes = pl.ds(tile * row_tile, row_tile)
        q = flat_rows(q_ref[pl.ds(t0, tile_tokens)]).astype(jnp.bfloat16)
        g32 = flat_rows(g_ref[pl.ds(t0, tile_tokens)])

        def score_step(c, top):
            s = dot(kv_chunk(0, c), q, NT) * to_log2
            blocks = chunk // BLK
            bias = bias_ref[0, pl.ds(c * blocks, blocks), :, lanes]
            s = (s.reshape(blocks, BLK, row_tile) + bias).reshape(chunk, row_tile)
            s_buf[pl.ds(c * chunk, chunk)] = s
            return jnp.maximum(top, jnp.max(s, axis=0, keepdims=True))

        top = for_chunks(count, score_step, jnp.full((1, row_tile), -jnp.inf, jnp.float32))

        def weight_step(c, carry):
            total, out_t = carry
            e = jnp.exp2(s_buf[pl.ds(c * chunk, chunk)] - top)
            total = total + jnp.sum(e, axis=0, keepdims=True)
            e16 = e.astype(jnp.bfloat16)
            e_buf[pl.ds(c * chunk, chunk)] = e16
            out_t = out_t + dot(kv_chunk(1, c).T, e16)
            return total, out_t

        total, out_t = for_chunks(
            count,
            weight_step,
            (jnp.zeros((1, row_tile), jnp.float32), jnp.zeros((width, row_tile), jnp.float32)),
        )
        inverse = 1.0 / total
        out16 = (out_t * inverse).T.astype(jnp.bfloat16)
        out32 = out16.astype(jnp.float32)
        out_ref[pl.ds(t0, tile_tokens)] = out32.reshape(tile_tokens, group, width).astype(jnp.bfloat16)
        delta = jnp.sum((g32 * out32).T, axis=0, keepdims=True) * inverse
        g16 = (g32.T * inverse).T.astype(jnp.bfloat16)

        def grad_step(c, dq_t):
            at = pl.ds(c * chunk, chunk)
            e16 = e_buf[at]
            dp = dot(kv_chunk(1, c), g16, NT)
            ds = (e16.astype(jnp.float32) * (dp - delta)).astype(jnp.bfloat16)
            dk = dot(ds, q)
            dv = dot(e16, g16)
            if tile > 0:
                dk = dk + acc[0, at]
                dv = dv + acc[1, at]
            if tile < tiles - 1:
                acc[0, at] = dk
                acc[1, at] = dv
            else:
                shape = (per_chunk, shard_tokens, width)
                spot = pl.ds(c * per_chunk, per_chunk)
                dkv_ref[spot, 0, 0] = (dk * factor).astype(jnp.bfloat16).reshape(shape)
                dkv_ref[spot, 0, 1] = dv.astype(jnp.bfloat16).reshape(shape)
            return dq_t + dot(kv_chunk(0, c).T, ds)

        dq_t = for_chunks(count, grad_step, jnp.zeros((width, row_tile), jnp.float32))
        dq = (dq_t * factor).T.reshape(tile_tokens, group, width)
        dq_ref[pl.ds(t0, tile_tokens)] = dq.astype(jnp.bfloat16)


def local_attention(queries, out_grad, kv, bias):
    tokens, heads, width = queries.shape
    shards, kv_heads, _, shard_tokens, _ = kv.shape
    group = heads // kv_heads
    length = shards * shard_tokens
    rows = tokens * group
    chunk = math.gcd(length, 256)
    row_tile = rows
    while row_tile * length > (1 << 21) and row_tile > 128:
        row_tile //= 2
    acc_rows = length if row_tile < rows else 8
    blocks = length // BLK
    q_spec = pl.BlockSpec((tokens, group, width), lambda g: (0, g, 0))
    kv_spec = pl.BlockSpec((shards, 1, 2, shard_tokens, width), lambda g: (0, g, 0, 0, 0))
    return pl.pallas_call(
        functools.partial(attention, (chunk, row_tile)),
        grid=(kv_heads,),
        in_specs=[
            q_spec,
            q_spec,
            kv_spec,
            pl.BlockSpec((1, blocks, 1, rows), lambda g: (g, 0, 0, 0)),
        ],
        out_specs=[q_spec, q_spec, kv_spec],
        out_shape=[
            jax.ShapeDtypeStruct(queries.shape, jnp.bfloat16),
            jax.ShapeDtypeStruct(queries.shape, jnp.bfloat16),
            jax.ShapeDtypeStruct(kv.shape, jnp.bfloat16),
        ],
        scratch_shapes=[
            pltpu.VMEM((length, row_tile), jnp.float32),
            pltpu.VMEM((length, row_tile), jnp.bfloat16),
            pltpu.VMEM((2, acc_rows, width), jnp.float32),
        ],
        compiler_params=pltpu.CompilerParams(vmem_limit_bytes=60 * 1024 * 1024),
        name="attention",
    )(queries, out_grad, kv, bias)


def row_bias(rand_all, global_blocks, first, here, block_count, kv_heads):
    heads = rand_all.shape[0]
    group = heads // kv_heads
    mine = lax.dynamic_slice_in_dim(rand_all, first, here, axis=1)
    ids = first + jnp.arange(here, dtype=jnp.int32)
    key_ids = jnp.arange(block_count, dtype=jnp.int32)
    away = (key_ids[None, :] - ids[:, None] + block_count + 1) % block_count
    common = (away <= 2) | jnp.any(key_ids[None, :, None] == global_blocks[None, None, :], axis=2)
    chosen = jnp.any(mine[:, :, None, :] == key_ids[None, None, :, None], axis=3)
    live = chosen | common[None]
    bias = jnp.where(live, 0.0, -jnp.inf).astype(jnp.float32)
    bias = bias.reshape(kv_heads, group, here, block_count).transpose(0, 3, 2, 1)
    bias = jnp.broadcast_to(bias[:, :, :, None, :], (kv_heads, block_count, here, BLK, group))
    return bias.reshape(kv_heads, block_count, 1, here * BLK * group)


def body(queries, keys, values, out_grad, rand_blocks, global_blocks):
    tokens, kv_heads, width = keys.shape
    here = tokens // BLK
    block_count = rand_blocks.shape[1]
    me = lax.axis_index("ctx")
    kv_here = jnp.stack([keys.transpose(1, 0, 2), values.transpose(1, 0, 2)], axis=1)
    kv = lax.all_gather(kv_here, "ctx", axis=0)
    rand_all = lax.all_gather(rand_blocks, "ctx", axis=0, tiled=True)
    bias = row_bias(rand_all, global_blocks, me * here, here, block_count, kv_heads)
    output, query_grad, parts = local_attention(queries, out_grad, kv, bias)
    sums = lax.psum_scatter(parts, "ctx", scatter_dimension=0, tiled=False)
    grads = sums.transpose(1, 2, 0, 3)
    return output, query_grad, grads[0], grads[1]


def solution(mesh):
    split = P(("dp", "ctx"), None, None)
    return jax.shard_map(
        body,
        mesh=mesh,
        in_specs=(split, split, split, split, split, P("dp")),
        out_specs=(split, split, split, split),
        check_vma=False,
    )
```

time: 960 us -> 162 us (0.17)
  local copies, waits for them, and re-layouts: 305 us -> 16.5 us
  waiting for transfers between devices: 310 us -> 76.2 us
  other arithmetic: 151 us -> 2.75 us
  matrix products: 147 us -> 0 us
  starting transfers between devices: 37 us -> 0.08 us
  Pallas kernels: 0 us -> 35.7 us
  blocking collectives: 0 us -> 15.9 us
  between operations: 0.76 us -> 14.1 us
    all_to_all x8 -> x0, waiting for transfers between devices: 310 us -> none  [the longest x1 49 us: body(): lax.all_to_all(queries, 'ctx', split_axis=1, concat_axis=0, tiled=True)]
    dot_general x80 -> x0, matrix products: 137 us -> none  [contract(): return jnp.einsum(form, left, right, preferred_element_type=jnp.float32)]
    scatter-add x32 -> x0, other arithmetic: 119 us -> none  [the longest x16 59.7 us: backward_one_group(): key_acc = key_acc.at[flat_ids].add(key_part.reshape(-1, BLK, head_width))]
    dynamic_slice x104 -> x2, local copies, waits for them, and re-layouts: 102 us -> 0.18 us  [row_bias(): mine = lax.dynamic_slice_in_dim(rand_all, first, here, axis=1)]
    dynamic_update_slice x40 -> x0, local copies, waits for them, and re-layouts: 70.8 us -> none  [body(): lax.map(partial(forward_head, global_blocks), (query_lead, key_lead, valu...]
    reduce_scatter x0 -> x1, waiting for transfers between devices: none -> 48.3 us  [body(): sums = lax.psum_scatter(parts, 'ctx', scatter_dimension=0, tiled=False)]
    all_to_all x8 -> x0, starting transfers between devices: 37 us -> none  [the longest x1 6.49 us: body(): lax.all_to_all(queries, 'ctx', split_axis=1, concat_axis=0, tiled=True)]
    pallas_call x0 -> x1, Pallas kernels: none -> 35.7 us  [local_attention(): pl.pallas_call(functools.partial(attention, (chunk, row_tile)), grid=(kv_...]
  transfers between devices with their start and end apart: 8 -> 2, of which waited for: 7 -> 2; matrix products, arithmetic and copies ran while one was open for 23% -> 5% of each run, Pallas kernels for 0% -> 0%
where the time goes in v1:
time: 162 us; the launch traced here: 161 us
  waiting for transfers between devices  76.2 us (47%)
  Pallas kernels  35.7 us (22%)
  local copies, waits for them, and re-layouts  16.5 us (10%)
  blocking collectives  15.9 us (10%)
  between operations  14.1 us (9%)
  other arithmetic  2.75 us (2%)
    reduce_scatter x1, waiting for transfers between devices, body(): sums = lax.psum_scatter(parts, 'ctx', scatter_dimension=0, tiled=False)  48.3 us
    pallas_call x1, Pallas kernels, local_attention(): pl.pallas_call(functools.partial(attention, (chunk, row_tile)), grid=(kv_...  35.7 us
    all_gather x1, waiting for transfers between devices, body(): kv = lax.all_gather(kv_here, 'ctx', axis=0)  27.9 us
    all_gather x1, blocking collectives, body(): rand_all = lax.all_gather(rand_blocks, 'ctx', axis=0, tiled=True)  15.9 us
    all_gather x1, local copies, waits for them, and re-layouts, body(): kv = lax.all_gather(kv_here, 'ctx', axis=0)  6.86 us
    reshape x1, local copies, waits for them, and re-layouts, row_bias(): return bias.reshape(kv_heads, block_count, 1, here * BLK * group)  4.25 us
  transfers between devices with their start and end apart: 2, of which 2 were waited for; matrix products, arithmetic and copies ran while one was open for 5% of the time, Pallas kernels for 0%

profile of v1, /device:TPU:0, one launch (start us, length us, event | category | flops | bytes accessed | tf_op | source)
XLA Modules:
  0.0 161.2 jit_solution(257455382485260402)
XLA Ops:
  7.2 0.0 all-gather.3.cloned.1.call-start
  7.2 1.9 %pad_maximum_fusion = bf16[8,2,128,128]{3,0,2,1:T(8,128)(2,1)} fusion(bf16[8,1,128,128]{3,0,2,1:T(8,128)(2,1)} %bitcast.24, bf16[8,1,128,128]{3,0,2,1:T(8,128)(2,1)} %bitcast.25), kind=kLoop, calls=%fused_computation | loop fusion | flops 262144 | bytes 1048576 | tf_op jit(solution)/shard_map/stack | solution.py:167
  9.1 0.0 all-gather.3.cloned.1.call-update
  9.1 0.0 reduce-scatter.2.cloned.1.call-start
  9.2 15.9 %all_gather.11 = s32[64,16,3]{1,0,2:T(8,128)S(1)} all-gather(s32[8,16,3]{1,0,2:T(8,128)} %param.10), channel_id=1, replica_groups=mesh['dp'=4,'ctx'=8] {'ctx'}, dimensions={0}, use_global_device_ids=true | all-gather | bytes 13824 | tf_op jit(solution)/shard_map/all_gather | solution.py:169
  25.1 0.1 constant_dynamic-slice_fusion
  25.2 0.1 copy.21
  25.3 0.1 copy.22
  25.4 0.7 compare_reduce_fusion
  26.1 0.1 compare_or_fusion
  26.3 2.2 %broadcast_in_dim.12 = f32[8,16,2,64,8]{1,4,3,2,0:T(8,128)} broadcast(f32[8,16,2,8]{1,3,2,0:T(8,128)S(1)} %copy.23), dimensions={0,1,2,4} | broadcast | bytes 532480 | tf_op jit(solution)/shard_map/broadcast_in_dim | solution.py:158
  28.5 4.2 %copy.24.bias_ref = f32[8,16,1,1024]{3,2,1,0:T(1,128)} copy(f32[8,16,1,1024]{1,3,0,2:T(8,128)} %bitcast.22) | data formatting | bytes 1048576 | tf_op jit(solution)/shard_map/reshape | solution.py:159
  32.8 27.9 %all-gather.3.cloned.1.call-done = bf16[64,2,128,128]{3,0,2,1:T(8,128)(2,1)} async-done(((bf16[8,2,128,128]{3,0,2,1:T(8,128)(2,1)}), bf16[64,2,128,128]{3,0,2,1:T(8,128)(2,1)}) %all-gather.3.cloned.1.call-update) | async-done | bytes 4194320 | tf_op jit(solution)/shard_map/all_gather | solution.py:168
  60.7 6.9 %copy.20 = bf16[64,2,128,128]{3,2,1,0:T(8,128)(2,1)} copy(bf16[64,2,128,128]{3,0,2,1:T(8,128)(2,1)} %all-gather.3.cloned.1.call-done) | data formatting | bytes 8388608 | tf_op jit(solution)/shard_map/all_gather | solution.py:168
  67.5 35.7 %attention.1 = (bf16[128,64,128]{2,1,0:T(8,128)(2,1)}, bf16[128,64,128]{2,1,0:T(8,128)(2,1)}, bf16[8,8,2,128,128]{4,3,2,1,0:T(8,128)(2,1)}) custom-call(bf16[128,64,128]{2,1,0:T(8,128)(2,1)} %q_ref.1, bf16[128,64,128]{2,1,0:T(8,128)(2,1)} %g_ref.1, bf16[8,8,2,128,128]{4,3,2,1,0:T(8,128)(2,1)} %bitcast.21, f32[8,16,1,1024]{3,2,1,0:T(1,128)} %copy.24.bias_ref), custom_call_target="tpu_custom_call" | custom-call | tf_op jit(solution)/shard_map/attention/pallas_call | solution.py:121
  103.2 0.0 reduce-scatter.2.cloned.1.call-update
  103.3 48.3 %reduce-scatter.2.cloned.1.call-done = bf16[1,8,2,128,128]{4,3,2,1,0:T(8,128)(2,1)} async-done(((bf16[8,8,2,128,128]{4,3,2,1,0:T(8,128)(2,1)}), bf16[1,8,2,128,128]{4,3,2,1,0:T(8,128)(2,1)}) %reduce-scatter.2.cloned.1.call-update) | async-done | bytes 524304 | tf_op jit(solution)/shard_map/reduce_scatter | solution.py:172
  151.6 1.1 slice_bitcast_fusion
  152.6 0.9 copy.26
  153.5 0.9 copy.25
  (4 shorter events, 0.1 us)
Async XLA Ops:
  7.2 53.5 %all-gather.3.cloned.1.call-start = ((), (), s32[]{:S(2)}) async-start(), calls=%async_computation.2 | async-start | bytes 4718592 | tf_op jit(solution)/shard_map/all_gather | solution.py:168
  9.1 142.5 %reduce-scatter.2.cloned.1.call-start = ((), (), s32[]{:S(2)}) async-start(), calls=%async_computation.1 | async-start | bytes 4718592 | tf_op jit(solution)/shard_map/reduce_scatter | solution.py:172
Sparse Core Ops, SparseCore 0:
  10.1 50.4 all-gather.2
  103.4 48.1 reduce-scatter.1

commit v2 on v1

--- a/solution.py
+++ b/solution.py
@@ -159,11 +159,399 @@
     return bias.reshape(kv_heads, block_count, 1, here * BLK * group)
 
 
-def body(queries, keys, values, out_grad, rand_blocks, global_blocks):
+def fused_kernel(
+    ids_in, kv_in, q_hbm, g_hbm, out_hbm, dq_hbm, grads_ref,
+    q_buf, g_buf, o_buf, dq_buf, kv_buf, part_buf, sib_in, right_in, left_in, right_out, left_out,
+    ids_buf, bias_buf, s_buf, e_buf,
+    q_sem, g_sem, o_sem, dq_sem,
+    ids_send, ids_recv, sib_send, sib_recv, fwd_send, fwd_recv, back_send, back_recv,
+    pair_send, pair_recv, right_send, right_recv, left_send, left_recv,
+):
+    heads, _, chips, _, shard_tokens, width = kv_buf.shape
+    shards = 2 * chips
+    _, tokens, group, _ = q_buf.shape
+    rows = tokens * group
+    here = tokens // BLK
+    block_count = shards * here
+    half = BLK * group
+    factor = 1.0 / math.sqrt(width)
+    to_log2 = factor * math.log2(math.e)
+    me = lax.axis_index("ctx")
+    z, core = me // 2, me % 2
+    pair = z * 2 + 1 - core
+    ahead, behind = me + 2, me - 2
+    last = chips - 1
+
+    def send(source, target, send_sem, recv_sem, to):
+        return pltpu.make_async_remote_copy(
+            src_ref=source, dst_ref=target, send_sem=send_sem, recv_sem=recv_sem,
+            device_id={"ctx": to}, device_id_type=pl.DeviceIdType.MESH,
+        )
+
+    def send_ids(k):
+        to = lax.rem(me + k, shards)
+        return send(ids_in.at[to], ids_buf.at[me], ids_send.at[k], ids_recv.at[me], to)
+
+    def got_ids(k):
+        origin = lax.rem(me + k, shards)
+        return send(ids_in.at[origin], ids_buf.at[origin], ids_send.at[k], ids_recv.at[origin], origin)
+
+    def kv_move(h, origin, lane, sems, to):
+        spot = kv_buf.at[h, lane, origin]
+        return send(spot, spot, sems[0].at[h, origin], sems[1].at[h, origin], to)
+
+    sib_sems, fwd_sems, back_sems = (sib_send, sib_recv), (fwd_send, fwd_recv), (back_send, back_recv)
+
+    def pair_move(h):
+        return send(part_buf.at[h, 1 - core], sib_in.at[h], pair_send.at[h], pair_recv.at[h], pair)
+
+    def right_move(h, zd):
+        return send(right_out.at[h, zd], right_in.at[h, zd], right_send.at[h, zd], right_recv.at[h, zd], ahead)
+
+    def left_move(h, zd):
+        return send(left_out.at[h, zd], left_in.at[h, zd], left_send.at[h, zd], left_recv.at[h, zd], behind)
+
+    def head_columns(ref, h):
+        return ref.at[:, pl.ds(pl.multiple_of(h * group, group), group), :]
+
+    def load_q(h):
+        return pltpu.make_async_copy(head_columns(q_hbm, h), q_buf.at[h], q_sem.at[h])
+
+    def load_g(h):
+        return pltpu.make_async_copy(head_columns(g_hbm, h), g_buf.at[h], g_sem.at[h])
+
+    def store_o(h):
+        return pltpu.make_async_copy(o_buf.at[h], head_columns(out_hbm, h), o_sem.at[h])
+
+    def store_dq(h):
+        return pltpu.make_async_copy(dq_buf.at[h], head_columns(dq_hbm, h), dq_sem.at[h])
+
+    def each_head(step):
+        def run(h, carry):
+            step(h)
+            return carry
+        lax.fori_loop(0, heads, run, 0)
+
+    def start_loads(h):
+        load_q(h).start()
+        load_g(h).start()
+
+    def place_own(h):
+        kv_buf[h, core, z] = kv_in[h]
+
+    each_head(start_loads)
+    each_head(place_own)
+    ids_buf[me] = ids_in[me]
+
+    barrier = pltpu.get_barrier_semaphore()
+    for k in range(1, shards):
+        pl.semaphore_signal(
+            barrier, inc=1, device_id={"ctx": lax.rem(me + k, shards)}, device_id_type=pl.DeviceIdType.MESH
+        )
+    pl.semaphore_wait(barrier, shards - 1)
+
+    def forward_kv(h, origin, rightward, leftward):
+        @pl.when(rightward)
+        def _():
+            kv_move(h, origin, core, fwd_sems, ahead).start()
+
+        @pl.when(leftward)
+        def _():
+            kv_move(h, origin, core, back_sems, behind).start()
+
+        kv_move(h, origin, core, sib_sems, pair).start()
+
+    def both(h):
+        return part_buf[h, core].astype(jnp.float32), sib_in[h].astype(jnp.float32)
+
+    def combined(h, zd):
+        return part_buf[h, core, zd].astype(jnp.float32) + sib_in[h, zd].astype(jnp.float32)
+
+    def in_heads(h):
+        return jnp.logical_and(h >= 0, h < heads)
+
+    def reduce_right(h):
+        for zd in range(1, chips):
+            @pl.when(zd > z)
+            def _(zd=zd):
+                @pl.when(z == 0)
+                def _():
+                    right_out[h, zd] = combined(h, zd).astype(jnp.bfloat16)
+
+                @pl.when(z > 0)
+                def _():
+                    right_move(h, zd).wait_recv()
+                    total = combined(h, zd) + right_in[h, zd].astype(jnp.float32)
+                    right_out[h, zd] = total.astype(jnp.bfloat16)
+
+                right_move(h, zd).start()
+
+    def reduce_left(h):
+        for zd in range(chips - 1):
+            @pl.when(zd < z)
+            def _(zd=zd):
+                @pl.when(z == last)
+                def _():
+                    left_out[h, zd] = combined(h, zd).astype(jnp.bfloat16)
+
+                @pl.when(z < last)
+                def _():
+                    left_move(h, zd).wait_recv()
+                    total = combined(h, zd) + left_in[h, zd].astype(jnp.float32)
+                    left_out[h, zd] = total.astype(jnp.bfloat16)
+
+                left_move(h, zd).start()
+
+    def finish(h):
+        @pl.when(z > 0)
+        def _():
+            right_move(h, z).wait_recv()
+
+        @pl.when(z < last)
+        def _():
+            left_move(h, z).wait_recv()
+
+        @pl.when(z == 0)
+        def _():
+            grads_ref[h] = (combined(h, z) + left_in[h, z].astype(jnp.float32)).astype(jnp.bfloat16)
+
+        @pl.when(z == last)
+        def _():
+            grads_ref[h] = (combined(h, z) + right_in[h, z].astype(jnp.float32)).astype(jnp.bfloat16)
+
+        @pl.when(jnp.logical_and(z > 0, z < last))
+        def _():
+            arrived = right_in[h, z].astype(jnp.float32) + left_in[h, z].astype(jnp.float32)
+            grads_ref[h] = (combined(h, z) + arrived).astype(jnp.bfloat16)
+
+    def compute(h):
+        load_q(h).wait()
+        load_g(h).wait()
+        q = flat_rows(q_buf[h]).astype(jnp.bfloat16)
+        g32 = flat_rows(g_buf[h])
+        ids = ids_buf[h]
+        key_ids = lax.broadcasted_iota(jnp.int32, (block_count, ids.shape[1]), 0)
+        slots = (ids.shape[0] - 2) // here
+        for b in range(here):
+            away = key_ids - (me * here + b) + (block_count + 1)
+            for _ in range(2):
+                away = jnp.where(away >= block_count, away - block_count, away)
+            live = (away <= 2) | (key_ids == ids[6:7]) | (key_ids == ids[7:8])
+            for k in range(slots):
+                live = live | (key_ids == ids[b * slots + k:b * slots + k + 1])
+            bias = jnp.where(live, 0.0, -jnp.inf).astype(jnp.float32)
+            reps = half // ids.shape[1]
+            bias_buf[:, b * half:(b + 1) * half] = jnp.concatenate([bias] * reps, axis=1)
+
+        chunk = 2 * shard_tokens
+        spans = [(lane, zz) for lane in range(2) for zz in range(0, chips, 2)]
+
+        def kv_chunk(which, span):
+            return kv_buf[h, span[0], span[1]:span[1] + 2, which].reshape(chunk, width)
+
+        top = None
+        for c, span in enumerate(spans):
+            s = dot(kv_chunk(0, span), q, NT) * to_log2
+            pieces = []
+            for j in range(2 * here):
+                block = ((span[1] + j // here) * 2 + span[0]) * here + j % here
+                pieces.append(s[j * BLK:(j + 1) * BLK] + bias_buf[block:block + 1])
+            s = jnp.concatenate(pieces, axis=0)
+            s_buf[c * chunk:(c + 1) * chunk] = s
+            here_top = jnp.max(s, axis=0, keepdims=True)
+            top = here_top if top is None else jnp.maximum(top, here_top)
+
+        total = jnp.zeros((1, rows), jnp.float32)
+        out_t = jnp.zeros((width, rows), jnp.float32)
+        for c, span in enumerate(spans):
+            e = jnp.exp2(s_buf[c * chunk:(c + 1) * chunk] - top)
+            total = total + jnp.sum(e, axis=0, keepdims=True)
+            e16 = e.astype(jnp.bfloat16)
+            e_buf[c * chunk:(c + 1) * chunk] = e16
+            out_t = out_t + dot(kv_chunk(1, span).T, e16)
+        inverse = 1.0 / total
+        out16 = (out_t * inverse).T.astype(jnp.bfloat16)
+        out32 = out16.astype(jnp.float32)
+        o_buf[h] = out32.reshape(tokens, group, width).astype(jnp.bfloat16)
+        store_o(h).start()
+        delta = jnp.sum((g32 * out32).T, axis=0, keepdims=True) * inverse
+        g16 = (g32.T * inverse).T.astype(jnp.bfloat16)
+
+        dq_t = jnp.zeros((width, rows), jnp.float32)
+        for c, span in enumerate(spans):
+            e16 = e_buf[c * chunk:(c + 1) * chunk]
+            dp = dot(kv_chunk(1, span), g16, NT)
+            ds = (e16.astype(jnp.float32) * (dp - delta)).astype(jnp.bfloat16)
+            shape = (2, shard_tokens, width)
+            dk = (dot(ds, q) * factor).astype(jnp.bfloat16)
+            dv = dot(e16, g16).astype(jnp.bfloat16)
+            part_buf[h, span[0], span[1]:span[1] + 2, 0] = dk.reshape(shape)
+            part_buf[h, span[0], span[1]:span[1] + 2, 1] = dv.reshape(shape)
+            dq_t = dq_t + dot(kv_chunk(0, span).T, ds)
+        pair_move(h).start()
+        dq = (dq_t * factor).T.reshape(tokens, group, width)
+        dq_buf[h] = dq.astype(jnp.bfloat16)
+        store_dq(h).start()
+
+    lag = chips
+
+    def slot(t, carry):
+        for d in range(1, chips):
+            h = t - d
+
+            @pl.when(in_heads(h))
+            def _(h=h, d=d):
+                @pl.when(z - d >= 0)
+                def _():
+                    kv_move(h, z - d, core, fwd_sems, ahead).wait_recv()
+                    forward_kv(h, z - d, z < last, z < 0)
+
+                @pl.when(z + d <= last)
+                def _():
+                    kv_move(h, z + d, core, back_sems, behind).wait_recv()
+                    forward_kv(h, z + d, z < 0, z > 0)
+
+        @pl.when(t < heads)
+        def _():
+            forward_kv(t, z, z < last, z > 0)
+
+        @pl.when(t == 0)
+        def _():
+            for k in range(1, shards):
+                send_ids(k).start()
+
+        e = t - lag - 1
+
+        @pl.when(in_heads(e))
+        def _():
+            pair_move(e).wait_recv()
+
+        @pl.when(jnp.logical_and(in_heads(e - z), z < last))
+        def _():
+            reduce_right(e - z)
+
+        @pl.when(jnp.logical_and(in_heads(e - (last - z)), z > 0))
+        def _():
+            reduce_left(e - (last - z))
+
+        f = e - jnp.maximum(z, last - z)
+
+        @pl.when(in_heads(f))
+        def _():
+            finish(f)
+
+        @pl.when(t == lag)
+        def _():
+            for k in range(1, shards):
+                got_ids(k).wait_recv()
+
+        @pl.when(in_heads(t - lag))
+        def _():
+            for origin in range(chips):
+                kv_move(t - lag, origin, 1 - core, sib_sems, pair).wait_recv()
+            compute(t - lag)
+
+        return carry
+
+    lax.fori_loop(0, heads + lag + chips, slot, 0)
+
+    for k in range(1, shards):
+        send_ids(k).wait_send()
+
+    def drain(h):
+        store_o(h).wait()
+        store_dq(h).wait()
+        pair_move(h).wait_send()
+        for origin in range(chips):
+            kv_move(h, origin, core, sib_sems, pair).wait_send()
+
+            @pl.when(jnp.logical_and(origin <= z, z < last))
+            def _(origin=origin):
+                kv_move(h, origin, core, fwd_sems, ahead).wait_send()
+
+            @pl.when(jnp.logical_and(origin >= z, z > 0))
+            def _(origin=origin):
+                kv_move(h, origin, core, back_sems, behind).wait_send()
+
+            @pl.when(origin > z)
+            def _(origin=origin):
+                right_move(h, origin).wait_send()
+
+            @pl.when(origin < z)
+            def _(origin=origin):
+                left_move(h, origin).wait_send()
+
+    each_head(drain)
+
+
+def fused(queries, out_grad, kv_here, ids):
+    tokens, heads, width = queries.shape
+    kv_heads = kv_here.shape[0]
+    group = heads // kv_heads
+    shards = ids.shape[0]
+    chips = shards // 2
+    rows = tokens * group
+    length = tokens * shards
+    bf16, f32 = jnp.bfloat16, jnp.float32
+    vmem = pl.BlockSpec(memory_space=pltpu.VMEM)
+    anywhere = pl.BlockSpec(memory_space=pl.ANY)
+    dma = pltpu.SemaphoreType.DMA
+    piece = (2, tokens, width)
+    block = pltpu.VMEM((kv_heads, tokens, group, width), bf16)
+    hop = pltpu.VMEM((kv_heads, chips) + piece, bf16)
+    return pl.pallas_call(
+        fused_kernel,
+        in_specs=[vmem, vmem, anywhere, anywhere],
+        out_specs=[anywhere, anywhere, vmem],
+        out_shape=[
+            jax.ShapeDtypeStruct(queries.shape, bf16),
+            jax.ShapeDtypeStruct(queries.shape, bf16),
+            jax.ShapeDtypeStruct(kv_here.shape, bf16),
+        ],
+        scratch_shapes=[block] * 4
+        + [pltpu.VMEM((kv_heads, 2, chips) + piece, bf16)] * 2
+        + [hop] * 5
+        + [
+            pltpu.VMEM(ids.shape, jnp.int32),
+            pltpu.VMEM((length // BLK, rows), f32),
+            pltpu.VMEM((length, rows), f32),
+            pltpu.VMEM((length, rows), bf16),
+        ]
+        + [dma((kv_heads,))] * 4
+        + [dma((shards,))] * 2
+        + [dma((kv_heads, chips))] * 6
+        + [dma((kv_heads,))] * 2
+        + [dma((kv_heads, chips))] * 4,
+        compiler_params=pltpu.CompilerParams(
+            collective_id=0, has_side_effects=True, vmem_limit_bytes=60 * 1024 * 1024
+        ),
+        name="fused",
+    )(ids, kv_here, queries, out_grad)
+
+
+def lane_ids(rand_blocks, global_blocks, shards, here):
+    group, block_count, slots = rand_blocks.shape
+    ids = rand_blocks.reshape(group, shards, here, slots).transpose(1, 2, 3, 0)
+    ids = ids.reshape(shards, here * slots, 1, group)
+    reps = 128 // group
+    ids = jnp.broadcast_to(ids, (shards, here * slots, reps, group)).reshape(shards, here * slots, 128)
+    common = jnp.broadcast_to(global_blocks[None, :, None], (shards, global_blocks.shape[0], 128))
+    return jnp.concatenate([ids, common], axis=1)
+
+
+def body(shards, queries, keys, values, out_grad, rand_blocks, global_blocks):
     tokens, kv_heads, width = keys.shape
     here = tokens // BLK
     block_count = rand_blocks.shape[1]
+    group = queries.shape[1] // kv_heads
     me = lax.axis_index("ctx")
+    if (shards == kv_heads == group == 8 and here == 2 and rand_blocks.shape[2] == 3
+            and global_blocks.shape[0] == 2):
+        kv_here = jnp.stack([keys.transpose(1, 0, 2), values.transpose(1, 0, 2)], axis=1)
+        ids = lane_ids(rand_blocks, global_blocks, shards, here)
+        output, query_grad, sums = fused(queries, out_grad, kv_here, ids)
+        grads = sums.transpose(1, 2, 0, 3)
+        return output, query_grad, grads[0], grads[1]
     kv_here = jnp.stack([keys.transpose(1, 0, 2), values.transpose(1, 0, 2)], axis=1)
     kv = lax.all_gather(kv_here, "ctx", axis=0)
     rand_all = lax.all_gather(rand_blocks, "ctx", axis=0, tiled=True)
@@ -177,7 +565,7 @@
 def solution(mesh):
     split = P(("dp", "ctx"), None, None)
     return jax.shard_map(
-        body,
+        functools.partial(body, mesh.shape["ctx"]),
         mesh=mesh,
         in_specs=(split, split, split, split, split, P("dp")),
         out_specs=(split, split, split, split),

time: 162 us -> 99.9 us (0.62)
  waiting for transfers between devices: 76.2 us -> 0 us
  Pallas kernels: 35.7 us -> 87.9 us
  blocking collectives: 15.9 us -> 0 us
  between operations: 14.1 us -> 0.68 us
  local copies, waits for them, and re-layouts: 16.5 us -> 9.52 us
    pallas_call x1, Pallas kernels: 35.7 us -> 87.9 us  [fused(): pl.pallas_call(fused_kernel, in_specs=[vmem, vmem, anywhere, anywhere], o...]
    reduce_scatter x1 -> x0, waiting for transfers between devices: 48.3 us -> none  [body(): sums = lax.psum_scatter(parts, 'ctx', scatter_dimension=0, tiled=False)]
    all_gather x1 -> x0, waiting for transfers between devices: 27.9 us -> none  [body(): kv = lax.all_gather(kv_here, 'ctx', axis=0)]
    all_gather x1 -> x0, blocking collectives: 15.9 us -> none  [body(): rand_all = lax.all_gather(rand_blocks, 'ctx', axis=0, tiled=True)]
    all_gather x1 -> x0, local copies, waits for them, and re-layouts: 6.86 us -> none  [body(): kv = lax.all_gather(kv_here, 'ctx', axis=0)]
    unnamed x2 -> x9, local copies, waits for them, and re-layouts: 1.75 us -> 6.2 us
    reshape x1 -> x2, local copies, waits for them, and re-layouts: 4.25 us -> 0.21 us  [lane_ids(): jnp.broadcast_to(ids, (shards, here * slots, reps, group))]
    broadcast_in_dim x1, local copies, waits for them, and re-layouts: 2.24 us -> 0.03 us  [lane_ids(): jnp.broadcast_to(ids, (shards, here * slots, reps, group))]
  transfers between devices with their start and end apart: 2 -> 0, of which waited for: 2 -> 0; matrix products, arithmetic and copies ran while one was open for 5% -> 0% of each run, Pallas kernels for 0% -> 0%
where the time goes in v2:
time: 99.9 us; the launch traced here: 99.6 us
  Pallas kernels  87.9 us (88%)
  local copies, waits for them, and re-layouts  9.52 us (10%)
  other arithmetic  1.53 us (2%)
    pallas_call x1, Pallas kernels, fused(): pl.pallas_call(fused_kernel, in_specs=[vmem, vmem, anywhere, anywhere], o...  87.9 us
    unnamed x9, local copies, waits for them, and re-layouts  6.2 us

profile of v2, /device:TPU:0, one launch (start us, length us, event | category | flops | bytes accessed | tf_op | source)
XLA Modules:
  0.0 99.6 jit_solution(17672923669310332998)
XLA Ops:
  0.6 0.7 pad.3.clone
  1.4 0.8 copy.14
  2.2 0.2 reshape.18
  2.4 0.7 pad_add_fusion.ids_in
  3.1 1.1 %copy_bitcast_fusion = (bf16[8,1,128,128]{3,2,1,0:T(8,128)(2,1)S(1)}, bf16[8,1,128,128]{3,2,1,0:T(8,128)(2,1)S(1)}) fusion(bf16[128,8,128]{2,1,0:T(8,128)(2,1)} %param.8, bf16[128,8,128]{2,1,0:T(8,128)(2,1)} %param.7), kind=kLoop, calls=%fused_computation.3 | loop fusion | bytes 1048576 | tf_op jit(solution)/shard_map/stack | solution.py:550
  4.2 0.8 pad_maximum_fusion.kv_in
  5.1 87.9 %fused.1 = (bf16[128,64,128]{2,1,0:T(8,128)(2,1)}, bf16[128,64,128]{2,1,0:T(8,128)(2,1)}, bf16[8,2,128,128]{3,2,1,0:T(8,128)(2,1)}) custom-call(s32[8,8,128]{2,1,0:T(8,128)} %pad_add_fusion.ids_in, bf16[8,2,128,128]{3,2,1,0:T(8,128)(2,1)} %pad_maximum_fusion.kv_in, bf16[128,64,128]{2,1,0:T(8,128)(2,1)} %q_hbm.1, bf16[128,64,128]{2,1,0:T(8,128)(2,1)} %g_hbm.1), custom_call_target="tpu_custom_call" | custom-call | tf_op jit(solution)/shard_map/fused/pallas_call | solution.py:502
  93.0 0.0 copy-start.1
  93.0 1.2 %slice_bitcast_fusion = (bf16[128,8,128]{2,0,1:T(8,128)(2,1)S(1)}, bf16[128,8,128]{2,0,1:T(8,128)(2,1)S(1)}) fusion(bf16[2,128,8,128]{3,1,0,2:T(8,128)(2,1)} %bitcast.21), kind=kLoop, calls=%fused_computation.1 | loop fusion | bytes 1048576 | tf_op jit(solution)/shard_map/squeeze | solution.py:554
  94.2 0.9 copy.20
  95.1 0.9 copy.19
  96.0 0.0 copy-done.1
  96.0 0.0 copy-start
  96.0 1.3 %copy.25 = bf16[128,64,128]{2,1,0:T(8,128)(2,1)} copy(bf16[128,64,128]{2,1,0:T(8,128)(2,1)S(1)} %copy-done.1) | data formatting | bytes 4194304
  97.3 1.0 %copy-done = bf16[128,64,128]{2,1,0:T(8,128)(2,1)S(1)} copy-done((bf16[128,64,128]{2,1,0:T(8,128)(2,1)S(1)}, bf16[128,64,128]{2,1,0:T(8,128)(2,1)}, u32[]{:S(2)}) %copy-start) | copy-done | bytes 2097176
  98.3 1.3 %copy.26 = bf16[128,64,128]{2,1,0:T(8,128)(2,1)} copy(bf16[128,64,128]{2,1,0:T(8,128)(2,1)S(1)} %copy-done) | data formatting | bytes 4194304
  (3 shorter events, 0.0 us)
Async XLA Ops:
  93.0 3.0 %copy-start.1 = (bf16[128,64,128]{2,1,0:T(8,128)(2,1)S(1)}, bf16[128,64,128]{2,1,0:T(8,128)(2,1)}, u32[]{:S(2)}) copy-start(bf16[128,64,128]{2,1,0:T(8,128)(2,1)} %get-tuple-element.26) | copy-start | bytes 6291460
  96.0 2.3 %copy-start = (bf16[128,64,128]{2,1,0:T(8,128)(2,1)S(1)}, bf16[128,64,128]{2,1,0:T(8,128)(2,1)}, u32[]{:S(2)}) copy-start(bf16[128,64,128]{2,1,0:T(8,128)(2,1)} %get-tuple-element.27) | copy-start | bytes 6291460

commit v3 on v2

--- a/solution.py
+++ b/solution.py
@@ -160,7 +160,7 @@
 
 
 def fused_kernel(
-    ids_in, kv_in, q_hbm, g_hbm, out_hbm, dq_hbm, grads_ref,
+    ids_in, k_in, v_in, q_hbm, g_hbm, out_hbm, dq_hbm, dk_ref, dv_ref, grads_ref,
     q_buf, g_buf, o_buf, dq_buf, kv_buf, part_buf, sib_in, right_in, left_in, right_out, left_out,
     ids_buf, bias_buf, s_buf, e_buf,
     q_sem, g_sem, o_sem, dq_sem,
@@ -236,11 +236,10 @@
         load_q(h).start()
         load_g(h).start()
 
-    def place_own(h):
-        kv_buf[h, core, z] = kv_in[h]
-
     each_head(start_loads)
-    each_head(place_own)
+    for which, ref in enumerate((k_in, v_in)):
+        turned = jnp.swapaxes(ref[...].astype(jnp.float32), 0, 1)
+        kv_buf[:, core, z, which] = turned.astype(jnp.bfloat16)
     ids_buf[me] = ids_in[me]
 
     barrier = pltpu.get_barrier_semaphore()
@@ -271,7 +270,7 @@
         return jnp.logical_and(h >= 0, h < heads)
 
     def reduce_right(h):
-        for zd in range(1, chips):
+        for zd in range(chips - 1, 0, -1):
             @pl.when(zd > z)
             def _(zd=zd):
                 @pl.when(z == 0)
@@ -393,10 +392,10 @@
         dq_buf[h] = dq.astype(jnp.bfloat16)
         store_dq(h).start()
 
-    lag = chips
+    lag = chips - 1
 
     def slot(t, carry):
-        for d in range(1, chips):
+        for d in range(chips - 1, 0, -1):
             h = t - d
 
             @pl.when(in_heads(h))
@@ -455,6 +454,10 @@
 
     lax.fori_loop(0, heads + lag + chips, slot, 0)
 
+    for which, ref in enumerate((dk_ref, dv_ref)):
+        turned = jnp.swapaxes(grads_ref[:, which].astype(jnp.float32), 0, 1)
+        ref[...] = turned.astype(jnp.bfloat16)
+
     for k in range(1, shards):
         send_ids(k).wait_send()
 
@@ -484,9 +487,9 @@
     each_head(drain)
 
 
-def fused(queries, out_grad, kv_here, ids):
+def fused(queries, out_grad, keys, values, ids):
     tokens, heads, width = queries.shape
-    kv_heads = kv_here.shape[0]
+    kv_heads = keys.shape[1]
     group = heads // kv_heads
     shards = ids.shape[0]
     chips = shards // 2
@@ -501,14 +504,15 @@
     hop = pltpu.VMEM((kv_heads, chips) + piece, bf16)
     return pl.pallas_call(
         fused_kernel,
-        in_specs=[vmem, vmem, anywhere, anywhere],
-        out_specs=[anywhere, anywhere, vmem],
+        in_specs=[vmem, vmem, vmem, anywhere, anywhere],
+        out_specs=[anywhere, anywhere, vmem, vmem],
         out_shape=[
             jax.ShapeDtypeStruct(queries.shape, bf16),
             jax.ShapeDtypeStruct(queries.shape, bf16),
-            jax.ShapeDtypeStruct(kv_here.shape, bf16),
+            jax.ShapeDtypeStruct(keys.shape, bf16),
+            jax.ShapeDtypeStruct(keys.shape, bf16),
         ],
-        scratch_shapes=[block] * 4
+        scratch_shapes=[pltpu.VMEM((kv_heads,) + piece, bf16)] + [block] * 4
         + [pltpu.VMEM((kv_heads, 2, chips) + piece, bf16)] * 2
         + [hop] * 5
         + [
@@ -526,7 +530,7 @@
             collective_id=0, has_side_effects=True, vmem_limit_bytes=60 * 1024 * 1024
         ),
         name="fused",
-    )(ids, kv_here, queries, out_grad)
+    )(ids, keys, values, queries, out_grad)
 
 
 def lane_ids(rand_blocks, global_blocks, shards, here):
@@ -547,11 +551,8 @@
     me = lax.axis_index("ctx")
     if (shards == kv_heads == group == 8 and here == 2 and rand_blocks.shape[2] == 3
             and global_blocks.shape[0] == 2):
-        kv_here = jnp.stack([keys.transpose(1, 0, 2), values.transpose(1, 0, 2)], axis=1)
         ids = lane_ids(rand_blocks, global_blocks, shards, here)
-        output, query_grad, sums = fused(queries, out_grad, kv_here, ids)
-        grads = sums.transpose(1, 2, 0, 3)
-        return output, query_grad, grads[0], grads[1]
+        return fused(queries, out_grad, keys, values, ids)
     kv_here = jnp.stack([keys.transpose(1, 0, 2), values.transpose(1, 0, 2)], axis=1)
     kv = lax.all_gather(kv_here, "ctx", axis=0)
     rand_all = lax.all_gather(rand_blocks, "ctx", axis=0, tiled=True)

time: 99.9 us -> 90.4 us (0.905)
  Pallas kernels: 87.9 us -> 81.1 us
  local copies, waits for them, and re-layouts: 9.52 us -> 7.72 us
    pallas_call x1, Pallas kernels: 87.9 us -> 81.1 us  [fused(): pl.pallas_call(fused_kernel, in_specs=[vmem, vmem, vmem, anywhere, anywhe...]
    squeeze x1 -> x0, local copies, waits for them, and re-layouts: 1.22 us -> none  [body(): return (output, query_grad, grads[0], grads[1])]
    another operation x1 -> x0, local copies, waits for them, and re-layouts: 1.12 us -> none  [body(): jnp.stack([keys.transpose(1, 0, 2), values.transpose(1, 0, 2)], axis=1)]
    unnamed x9 -> x11, local copies, waits for them, and re-layouts: 6.2 us -> 6.74 us
where the time goes in v3:
time: 90.4 us; the launch traced here: 90.1 us
  Pallas kernels  81.1 us (90%)
  local copies, waits for them, and re-layouts  7.72 us (9%)
    pallas_call x1, Pallas kernels, fused(): pl.pallas_call(fused_kernel, in_specs=[vmem, vmem, vmem, anywhere, anywhe...  81.1 us
    unnamed x11, local copies, waits for them, and re-layouts  6.74 us

profile of v3, /device:TPU:0, one launch (start us, length us, event | category | flops | bytes accessed | tf_op | source)
XLA Modules:
  0.0 90.1 jit_solution(2670144122571819589)
XLA Ops:
  0.6 0.7 pad.1.clone
  1.4 0.8 copy.10
  2.2 0.2 reshape.18
  2.4 0.7 pad_add_fusion.ids_in
  3.1 81.1 %fused.1 = (bf16[128,64,128]{2,1,0:T(8,128)(2,1)}, bf16[128,64,128]{2,1,0:T(8,128)(2,1)}, bf16[128,8,128]{2,1,0:T(8,128)(2,1)}, bf16[128,8,128]{2,1,0:T(8,128)(2,1)}) custom-call(s32[8,8,128]{2,1,0:T(8,128)} %pad_add_fusion.ids_in, bf16[128,8,128]{2,1,0:T(8,128)(2,1)} %k_in.1, bf16[128,8,128]{2,1,0:T(8,128)(2,1)} %v_in.1, bf16[128,64,128]{2,1,0:T(8,128)(2,1)} %q_hbm.1, ...), custom_call_target="tpu_custom_call" | custom-call | tf_op jit(solution)/shard_map/fused/pallas_call | solution.py:505
  84.2 0.0 copy-start
  84.2 3.2 %copy.17 = bf16[128,64,128]{2,1,0:T(8,128)(2,1)} copy(bf16[128,64,128]{2,1,0:T(8,128)(2,1)} %get-tuple-element.8) | data formatting | bytes 4194304
  87.4 0.0 copy-done
  87.4 0.0 copy-start.2
  87.4 0.0 copy-start.1
  87.4 1.3 %copy.18 = bf16[128,64,128]{2,1,0:T(8,128)(2,1)} copy(bf16[128,64,128]{2,1,0:T(8,128)(2,1)S(1)} %copy-done) | data formatting | bytes 4194304
  88.7 0.0 copy-done.2
  88.7 0.7 copy.19
  89.4 0.0 copy-done.1
  89.4 0.7 copy.20
  (3 shorter events, 0.0 us)
Async XLA Ops:
  84.2 3.2 %copy-start = (bf16[128,64,128]{2,1,0:T(8,128)(2,1)S(1)}, bf16[128,64,128]{2,1,0:T(8,128)(2,1)}, u32[]{:S(2)}) copy-start(bf16[128,64,128]{2,1,0:T(8,128)(2,1)} %get-tuple-element.9) | copy-start | bytes 6291460
  87.4 1.3 %copy-start.2 = (bf16[128,8,128]{2,1,0:T(8,128)(2,1)S(1)}, bf16[128,8,128]{2,1,0:T(8,128)(2,1)}, u32[]{:S(2)}) copy-start(bf16[128,8,128]{2,1,0:T(8,128)(2,1)} %get-tuple-element.10) | copy-start | bytes 786436
  87.4 2.0 %copy-start.1 = (bf16[128,8,128]{2,1,0:T(8,128)(2,1)S(1)}, bf16[128,8,128]{2,1,0:T(8,128)(2,1)}, u32[]{:S(2)}) copy-start(bf16[128,8,128]{2,1,0:T(8,128)(2,1)} %get-tuple-element.11) | copy-start | bytes 786436

commit v4 on v3

--- a/solution.py
+++ b/solution.py
@@ -377,8 +377,12 @@
         g16 = (g32.T * inverse).T.astype(jnp.bfloat16)
 
         dq_t = jnp.zeros((width, rows), jnp.float32)
-        for c, span in enumerate(spans):
-            e16 = e_buf[c * chunk:(c + 1) * chunk]
+        for k, zz in [(k, zz) for k in range(2) for zz in range(0, chips, 2)]:
+            if (k, zz) == (1, 0):
+                pair_move(h).start()
+            span = ((1 - core) if k == 0 else core, zz)
+            start = pl.multiple_of((span[0] * (chips // 2) + zz // 2) * chunk, chunk)
+            e16 = e_buf[pl.ds(start, chunk)]
             dp = dot(kv_chunk(1, span), g16, NT)
             ds = (e16.astype(jnp.float32) * (dp - delta)).astype(jnp.bfloat16)
             shape = (2, shard_tokens, width)
@@ -387,7 +391,6 @@
             part_buf[h, span[0], span[1]:span[1] + 2, 0] = dk.reshape(shape)
             part_buf[h, span[0], span[1]:span[1] + 2, 1] = dv.reshape(shape)
             dq_t = dq_t + dot(kv_chunk(0, span).T, ds)
-        pair_move(h).start()
         dq = (dq_t * factor).T.reshape(tokens, group, width)
         dq_buf[h] = dq.astype(jnp.bfloat16)
         store_dq(h).start()

time: 90.4 us -> 89 us (0.985)
  Pallas kernels: 81.1 us -> 79.7 us
    pallas_call x1, Pallas kernels: 81.1 us -> 79.7 us  [fused(): pl.pallas_call(fused_kernel, in_specs=[vmem, vmem, vmem, anywhere, anywhe...]
where the time goes in v4:
time: 89 us; the launch traced here: 88.8 us
  Pallas kernels  79.7 us (90%)
  local copies, waits for them, and re-layouts  7.72 us (9%)
    pallas_call x1, Pallas kernels, fused(): pl.pallas_call(fused_kernel, in_specs=[vmem, vmem, vmem, anywhere, anywhe...  79.7 us
    unnamed x11, local copies, waits for them, and re-layouts  6.74 us

profile of v4, /device:TPU:0, one launch (start us, length us, event | category | flops | bytes accessed | tf_op | source)
XLA Modules:
  0.0 88.8 jit_solution(15414850536884035890)
XLA Ops:
  0.6 0.7 pad.1.clone
  1.4 0.8 copy.10
  2.2 0.2 reshape.18
  2.4 0.7 pad_add_fusion.ids_in
  3.1 79.7 %fused.1 = (bf16[128,64,128]{2,1,0:T(8,128)(2,1)}, bf16[128,64,128]{2,1,0:T(8,128)(2,1)}, bf16[128,8,128]{2,1,0:T(8,128)(2,1)}, bf16[128,8,128]{2,1,0:T(8,128)(2,1)}) custom-call(s32[8,8,128]{2,1,0:T(8,128)} %pad_add_fusion.ids_in, bf16[128,8,128]{2,1,0:T(8,128)(2,1)} %k_in.1, bf16[128,8,128]{2,1,0:T(8,128)(2,1)} %v_in.1, bf16[128,64,128]{2,1,0:T(8,128)(2,1)} %q_hbm.1, ...), custom_call_target="tpu_custom_call" | custom-call | tf_op jit(solution)/shard_map/fused/pallas_call | solution.py:508
  82.8 0.0 copy-start
  82.8 3.2 %copy.17 = bf16[128,64,128]{2,1,0:T(8,128)(2,1)} copy(bf16[128,64,128]{2,1,0:T(8,128)(2,1)} %get-tuple-element.8) | data formatting | bytes 4194304
  86.0 0.0 copy-done
  86.0 0.0 copy-start.2
  86.0 0.0 copy-start.1
  86.0 1.3 %copy.18 = bf16[128,64,128]{2,1,0:T(8,128)(2,1)} copy(bf16[128,64,128]{2,1,0:T(8,128)(2,1)S(1)} %copy-done) | data formatting | bytes 4194304
  87.3 0.0 copy-done.2
  87.4 0.7 copy.19
  88.1 0.0 copy-done.1
  88.1 0.7 copy.20
  (3 shorter events, 0.0 us)
Async XLA Ops:
  82.8 3.2 %copy-start = (bf16[128,64,128]{2,1,0:T(8,128)(2,1)S(1)}, bf16[128,64,128]{2,1,0:T(8,128)(2,1)}, u32[]{:S(2)}) copy-start(bf16[128,64,128]{2,1,0:T(8,128)(2,1)} %get-tuple-element.9) | copy-start | bytes 6291460
  86.0 1.3 %copy-start.2 = (bf16[128,8,128]{2,1,0:T(8,128)(2,1)S(1)}, bf16[128,8,128]{2,1,0:T(8,128)(2,1)}, u32[]{:S(2)}) copy-start(bf16[128,8,128]{2,1,0:T(8,128)(2,1)} %get-tuple-element.10) | copy-start | bytes 786436
  86.0 2.0 %copy-start.1 = (bf16[128,8,128]{2,1,0:T(8,128)(2,1)S(1)}, bf16[128,8,128]{2,1,0:T(8,128)(2,1)}, u32[]{:S(2)}) copy-start(bf16[128,8,128]{2,1,0:T(8,128)(2,1)} %get-tuple-element.11) | copy-start | bytes 786436
